TPU v7x, 32 devices: a whole 2x2x4 slice. The times are simulated.
32 devices in a mesh: dp: 8 (over y, x, core), fsdp: 4 (over z).
Axes of the slice: x: 2, y: 2, z: 4, core: 2. Of those that a mesh axis runs over, the one named last changes fastest.
Arguments:
- teacher_in: bfloat16 [8, 512, 4096], P('dp', 'fsdp'), may hold values from -6 to 6
- teacher_out: bfloat16 [8, 512, 4096], P('dp', 'fsdp'), may hold values from -6 to 6
- owner_section: int32 [4], P('fsdp'), may hold values from 0 to 7
- gate_blocks: bfloat16 [32, 10, 128, 128], P('dp', None, 'fsdp'), may hold values from -0.15625 to 0.15625
- up_blocks: bfloat16 [32, 10, 128, 128], P('dp', None, 'fsdp'), may hold values from -0.15625 to 0.15625
- down_blocks: bfloat16 [32, 10, 128, 128], P('dp', None, 'fsdp'), may hold values from -0.15625 to 0.15625
- input_lists: int32 [32, 10], P('dp'), may hold values from 0 to 31, as said below
- input_counts: int32 [32], P('dp'), may hold values from 6 to 10, as said below
- output_lists: int32 [32, 10], P('dp'), may hold values from 0 to 31, as said below
- output_counts: int32 [32], P('dp'), may hold values from 6 to 10, as said below
Outputs:
- grad_gate: bfloat16 [32, 10, 128, 128], P('dp', None, 'fsdp')
- grad_up: bfloat16 [32, 10, 128, 128], P('dp', None, 'fsdp')
- grad_down: bfloat16 [32, 10, 128, 128], P('dp', None, 'fsdp')
Inputs may be any that keep to these rules, and one draw needn't show every extreme that they name: `input_lists`: the first 10 entries of each row are distinct; entries at dead slots are ignored. `input_counts`: among the hidden blocks of one index of dp, one block has exactly 10 live slots. `output_lists`: the first 10 entries of each row are distinct; entries at dead slots are ignored. `output_counts`: among the hidden blocks of one index of dp, one block has exactly 10 live slots.
All inputs are finite; a program needn't handle non-finite values.
Results may differ from a plain program's by a relative error of at most 0.025.
Values may be sent and summed in bfloat16 or wider, within the bound.
No kernel may reach another device: no remote copies, remote signals or barrier semaphores. Data moves between devices by JAX's collectives and lax.ppermute only.
A program may use at most 64 MiB of HBM per device.

v0:
```python
import jax
import jax.numpy as jnp
from jax import lax
from jax.sharding import PartitionSpec as P


def broadcast(shard, axis, root):
    mine = lax.axis_index(axis) == root
    return lax.psum(jnp.where(mine, shard, jnp.zeros_like(shard)), axis)


def live_mask(counts, slot_count):
    positions = jnp.arange(slot_count, dtype=jnp.int32)
    return (positions[None, :] < counts[:, None])[:, :, None, None]


def shards(
    teacher_in,
    teacher_out,
    owner_section,
    gate_blocks,
    up_blocks,
    down_blocks,
    input_lists,
    input_counts,
    output_lists,
    output_counts,
):
    root_section = owner_section[0]
    local_in = teacher_in[0]
    local_out = teacher_out[0]
    micro_count = lax.axis_size("fsdp")
    rows_in = broadcast(local_in, "dp", root_section)
    gate_full, up_full, down_full = (
        lax.all_gather(gate_blocks, "fsdp", axis=2, tiled=True),
        lax.all_gather(up_blocks, "fsdp", axis=2, tiled=True),
        lax.all_gather(down_blocks, "fsdp", axis=2, tiled=True),
    )
    slot_count = input_lists.shape[1]
    block_edge = gate_full.shape[3]
    tok_rows = rows_in.shape[0]
    model_width = rows_in.shape[1]
    row_blocks = model_width // block_edge
    input_live = live_mask(input_counts, slot_count)
    output_live = live_mask(output_counts, slot_count)
    zero_value = jnp.zeros((), jnp.bfloat16)
    gate_live = jnp.where(input_live, gate_full, zero_value)
    up_live = jnp.where(input_live, up_full, zero_value)
    down_live = jnp.where(output_live, down_full, zero_value)
    picked = rows_in.reshape(tok_rows, row_blocks, block_edge)[:, input_lists]
    gate_pre = jnp.einsum("tfki,fkio->tfo", picked, gate_live, preferred_element_type=jnp.float32)
    up_pre = jnp.einsum("tfki,fkio->tfo", picked, up_live, preferred_element_type=jnp.float32)
    sigmoid_gate = jax.nn.sigmoid(gate_pre)
    activated = gate_pre * sigmoid_gate
    hidden = (activated * up_pre).astype(jnp.bfloat16)
    pieces = jnp.einsum("tfi,fkio->tfko", hidden, down_live, preferred_element_type=jnp.float32)
    blank_out = jnp.zeros((tok_rows, row_blocks, block_edge), jnp.float32)
    partial_out = blank_out.at[:, output_lists].add(pieces).reshape(tok_rows, model_width)
    is_owner = lax.axis_index("dp") == root_section
    own_term = jnp.where(is_owner, local_out.astype(jnp.float32), jnp.float32(0.0))
    residual_rows = lax.psum((partial_out - own_term).astype(jnp.bfloat16), "dp").astype(
        jnp.float32
    )
    scaled_error = (residual_rows / micro_count).astype(jnp.bfloat16)
    error_picked = scaled_error.reshape(tok_rows, row_blocks, block_edge)[:, output_lists]
    output_scale = output_live.astype(jnp.float32)
    input_scale = input_live.astype(jnp.float32)
    down_grad = (
        jnp.einsum("tfi,tfko->fkio", hidden, error_picked, preferred_element_type=jnp.float32)
        * output_scale
    )
    hidden_grad = jnp.einsum(
        "tfko,fkio->tfi", error_picked, down_live, preferred_element_type=jnp.float32
    )
    gate_error = (
        hidden_grad * up_pre * sigmoid_gate * (1.0 + gate_pre * (1.0 - sigmoid_gate))
    ).astype(jnp.bfloat16)
    up_error = (hidden_grad * activated).astype(jnp.bfloat16)
    gate_grad = (
        jnp.einsum("tfki,tfo->fkio", picked, gate_error, preferred_element_type=jnp.float32)
        * input_scale
    )
    up_grad = (
        jnp.einsum("tfki,tfo->fkio", picked, up_error, preferred_element_type=jnp.float32)
        * input_scale
    )
    gate_sum, up_sum, down_sum = (
        lax.psum_scatter(
            gate_grad.astype(jnp.bfloat16), "fsdp", scatter_dimension=2, tiled=True
        ).astype(jnp.float32),
        lax.psum_scatter(
            up_grad.astype(jnp.bfloat16), "fsdp", scatter_dimension=2, tiled=True
        ).astype(jnp.float32),
        lax.psum_scatter(
            down_grad.astype(jnp.bfloat16), "fsdp", scatter_dimension=2, tiled=True
        ).astype(jnp.float32),
    )
    return (
        gate_sum.astype(jnp.bfloat16),
        up_sum.astype(jnp.bfloat16),
        down_sum.astype(jnp.bfloat16),
    )


def solution(mesh):
    return jax.shard_map(
        shards,
        mesh=mesh,
        in_specs=(
            P("dp", "fsdp", None),
            P("dp", "fsdp", None),
            P("fsdp"),
            P("dp", None, "fsdp", None),
            P("dp", None, "fsdp", None),
            P("dp", None, "fsdp", None),
            P("dp", None),
            P("dp"),
            P("dp", None),
            P("dp"),
        ),
        out_specs=(
            P("dp", None, "fsdp", None),
            P("dp", None, "fsdp", None),
            P("dp", None, "fsdp", None),
        ),
        check_vma=False,
    )
```

profile of v0, /device:TPU:0, one launch (start us, length us, event | category | flops | bytes accessed | tf_op | source)
XLA Modules:
  0.0 329.0 jit_solution(10549377895469457317)
XLA Ops:
  8.7 1.6 copy.63
  10.3 0.1 broadcast_select_fusion.3
  10.4 1.3 copy.64
  11.8 0.0 all-gather.6.cloned.1.call-start
  11.8 0.5 all-gather.6.cloned.1.call-update
  12.4 0.5 all-gather.8.cloned.1.call-update
  13.0 0.5 all-gather.4.cloned.1.call-update
  13.5 0.0 all-reduce.7.cloned.1.call-start
  13.6 0.1 reshape.108
  13.7 0.1 reshape.124
  13.8 1.3 copy.74
  15.1 0.1 iota_compare_fusion
  15.2 0.1 fusion.34
  15.3 56.3 %all-reduce.5.cloned.1.call-done = bf16[128,32,128]{2,0,1:T(8,128)(2,1)} async-done(((bf16[128,32,128]{2,0,1:T(8,128)(2,1)}), bf16[128,32,128]{2,0,1:T(8,128)(2,1)}) %all-reduce.5.cloned.1.call-update) | async-done | bytes 1048592 | tf_op jit(solution)/shard_map/psum | solution.py:9
  71.6 2.0 gather_fusion
  73.6 2.4 fusion.11
  76.1 5.8 %all-gather.8.cloned.1.call-done = bf16[4,10,128,128]{3,2,1,0:T(8,128)(2,1)} async-done(((bf16[4,10,32,128]{3,2,1,0:T(8,128)(2,1)}), bf16[4,10,128,128]{3,2,1,0:T(8,128)(2,1)}) %all-gather.8.cloned.1.call-update) | async-done | bytes 1310736 | tf_op jit(solution)/shard_map/all_gather | solution.py:36
  81.9 2.0 fusion.14
  83.9 0.1 fusion.23
  84.0 30.9 %all-gather.4.cloned.1.call-done = bf16[4,10,128,128]{3,2,1,0:T(8,128)(2,1)} async-done(((bf16[4,10,32,128]{3,2,1,0:T(8,128)(2,1)}), bf16[4,10,128,128]{3,2,1,0:T(8,128)(2,1)}) %all-gather.4.cloned.1.call-update) | async-done | bytes 1310736 | tf_op jit(solution)/shard_map/all_gather | solution.py:37
  114.9 2.0 fusion.17
  116.9 2.1 copy.72
  119.0 0.2 broadcast_in_dim.49
  119.2 6.5 %scatter_fusion = f32[128,32,128]{2,0,1:T(8,128)S(1)} fusion(f32[128,32,128]{2,0,1:T(8,128)S(1)} %broadcast_in_dim.49, s32[40]{0:T(128)S(1)} %reshape.124, f32[40,128,128]{2,1,0:T(8,128)} %copy.72), kind=kCustom, calls=%fused_computation.2 | custom fusion | flops 655360 | bytes 7864480 | tf_op jit(solution)/shard_map/scatter-add | solution.py:58
  125.8 1.8 copy.73
  127.6 2.9 fusion
  130.5 0.0 all-reduce.9.cloned.1.call-start
  130.6 56.0 %all-reduce.7.cloned.1.call-done = bf16[128,4096]{0,1:T(8,128)(2,1)} async-done(((bf16[128,4096]{0,1:T(8,128)(2,1)}), bf16[128,4096]{0,1:T(8,128)(2,1)}) %all-reduce.7.cloned.1.call-update) | async-done | bytes 1048592 | tf_op jit(solution)/shard_map/psum | solution.py:61
  186.5 1.4 multiply_convert_fusion.3
  188.0 0.7 copy.75
  188.6 0.8 gather_fusion.1
  189.4 0.8 copy.76
  190.2 1.6 fusion.1
  191.8 3.7 %copy.81 = bf16[4,10,128,128]{3,0,1,2:T(4,128)(2,1)} copy(bf16[4,10,128,128]{2,3,1,0:T(8,128)(2,1)} %fusion.1) | data formatting | bytes 2621440 | tf_op jit(solution)/shard_map/convert_element_type | solution.py:95
  195.6 0.0 reduce-scatter.3.cloned.1.call-start
  195.6 1.2 copy-done.1
  196.8 1.4 copy.65
  198.3 2.0 convolution_bitcast_fusion
  200.3 1.6 multiply_convert_fusion.2
  202.0 0.0 reduce-scatter.5.cloned.1.call-start
  202.0 1.6 multiply_convert_fusion.1
  203.6 0.6 copy-done.11
  204.3 0.6 dynamic-slice
  205.5 49.6 %all-reduce.9.cloned.1.call-done = bf16[4,10,128,128]{3,0,1,2:T(4,128)(2,1)} async-done(((bf16[4,10,128,128]{3,0,1,2:T(4,128)(2,1)}), bf16[4,10,128,128]{3,0,1,2:T(4,128)(2,1)}) %all-reduce.9.cloned.1.call-update) | async-done | bytes 1310736
  255.0 1.1 constant_dynamic-slice_fusion
  256.1 0.8 copy.82
  256.9 31.8 %reduce-scatter.3.cloned.1.call-done = bf16[4,10,32,128]{3,2,1,0:T(8,128)(2,1)} async-done(((bf16[4,10,128,128]{3,2,1,0:T(8,128)(2,1)}), bf16[4,10,32,128]{3,2,1,0:T(8,128)(2,1)}) %reduce-scatter.3.cloned.1.call-update) | async-done | bytes 327696 | tf_op jit(solution)/shard_map/reduce_scatter | solution.py:88
  288.7 32.9 %reduce-scatter.5.cloned.1.call-done = bf16[4,10,32,128]{3,2,1,0:T(8,128)(2,1)} async-done(((bf16[4,10,128,128]{3,2,1,0:T(8,128)(2,1)}), bf16[4,10,32,128]{3,2,1,0:T(8,128)(2,1)}) %reduce-scatter.5.cloned.1.call-update) | async-done | bytes 327696 | tf_op jit(solution)/shard_map/reduce_scatter | solution.py:91
  (35 shorter events, 0.3 us)
Async XLA Ops:
  8.0 63.6 %all-reduce.5.cloned.1.call-start = ((), (), s32[]{:S(2)}) async-start(), calls=%async_computation.2 | async-start | bytes 2097152 | tf_op jit(solution)/shard_map/psum | solution.py:9
  11.7 1.9 copy-start.7
  11.7 2.0 copy-start.8
  11.7 2.0 copy-start.4
  11.8 61.9 %all-gather.6.cloned.1.call-start = ((), (), s32[]{:S(2)}) async-start(), calls=%async_computation.4 | async-start | bytes 1638400 | tf_op jit(solution)/shard_map/all_gather | solution.py:35
  12.3 2.8 copy-start.9
  12.3 2.8 copy-start.10
  12.4 69.5 %all-gather.8.cloned.1.call-start = ((), (), s32[]{:S(2)}) async-start(), calls=%async_computation.5 | async-start | bytes 1638400 | tf_op jit(solution)/shard_map/all_gather | solution.py:36
  13.0 101.9 %all-gather.4.cloned.1.call-start = ((), (), s32[]{:S(2)}) async-start(), calls=%async_computation.3 | async-start | bytes 1638400 | tf_op jit(solution)/shard_map/all_gather | solution.py:37
  13.5 173.0 %all-reduce.7.cloned.1.call-start = ((), (), s32[]{:S(2)}) async-start(), calls=%async_computation.6 | async-start | bytes 2097152 | tf_op jit(solution)/shard_map/psum | solution.py:61
  73.6 8.3 %copy-start = (bf16[40,128,128]{2,1,0:T(8,128)(2,1)}, bf16[40,128,128]{2,1,0:T(8,128)(2,1)S(1)}, u32[]{:S(2)}) copy-start(bf16[40,128,128]{2,1,0:T(8,128)(2,1)S(1)} %gather_fusion) | copy-start | bytes 3932164
  83.9 31.0 %copy-start.5 = (f32[128,4,128]{0,2,1:T(8,128)}, f32[128,4,128]{0,2,1:T(8,128)S(1)}, u32[]{:S(2)}) copy-start(f32[128,4,128]{0,2,1:T(8,128)S(1)} %fusion.14) | copy-start | bytes 786436
  125.7 1.8 copy-start.2
  130.5 124.6 %all-reduce.9.cloned.1.call-start = ((), (), s32[]{:S(2)}) async-start(), calls=%async_computation.9 | async-start | bytes 2621440
  195.5 1.3 copy-start.1
  195.6 93.1 %reduce-scatter.3.cloned.1.call-start = ((), (), s32[]{:S(2)}) async-start(), calls=%async_computation.7 | async-start | bytes 1638400 | tf_op jit(solution)/shard_map/reduce_scatter | solution.py:88
  198.3 2.0 copy-start.3
  198.3 2.0 copy-start.6
  202.0 119.6 %reduce-scatter.5.cloned.1.call-start = ((), (), s32[]{:S(2)}) async-start(), calls=%async_computation.8 | async-start | bytes 1638400 | tf_op jit(solution)/shard_map/reduce_scatter | solution.py:91
  203.6 0.7 copy-start.11
Sparse Core Ops, SparseCore 0:
  12.0 59.5 all-reduce.4
  130.6 55.8 all-reduce.6
Sparse Core Ops, SparseCore 1:
  13.8 35.1 all-gather.5
  50.4 31.4 all-gather.7
  83.3 31.5 all-gather.3
  195.6 59.3 all-reduce.8
  257.9 30.7 reduce-scatter.2
  291.6 29.9 reduce-scatter.4
where the time goes:
time: 330 us; the launch traced here: 329 us
  waiting for transfers between devices  265 us (80%)
  local copies, waits for them, and re-layouts  22.4 us (7%)
  between operations  17.1 us (5%)
  matrix products  13.2 us (4%)
  other arithmetic  11.2 us (3%)
    psum x1, waiting for transfers between devices, broadcast(): return lax.psum(jnp.where(mine, shard, jnp.zeros_like(shard)), axis)  56.3 us
    psum x1, waiting for transfers between devices, shards(): lax.psum((partial_out - own_term).astype(jnp.bfloat16), 'dp')  56 us
    unnamed x9, waiting for transfers between devices  51.2 us
    reduce_scatter x1, waiting for transfers between devices, shards(): lax.psum_scatter(up_grad.astype(jnp.bfloat16), 'fsdp', scatter_dimension=...  32.9 us
    reduce_scatter x1, waiting for transfers between devices, shards(): lax.psum_scatter(gate_grad.astype(jnp.bfloat16), 'fsdp', scatter_dimensio...  31.8 us
    all_gather x1, waiting for transfers between devices, shards(): lax.all_gather(down_blocks, 'fsdp', axis=2, tiled=True)  30.9 us
    unnamed x29, local copies, waits for them, and re-layouts  7.28 us
  transfers between devices with their start and end apart: 8, of which 7 were waited for; matrix products, arithmetic and copies ran while one was open for 5% of the time, Pallas kernels for 0%

commit v1 on v0

--- a/solution.py
+++ b/solution.py
@@ -6,7 +6,7 @@
 
 def broadcast(shard, axis, root):
     mine = lax.axis_index(axis) == root
-    return lax.psum(jnp.where(mine, shard, jnp.zeros_like(shard)), axis)
+    return jnp.sum(lax.all_gather(jnp.where(mine, shard, jnp.zeros_like(shard)), axis), axis=0)
 
 
 def live_mask(counts, slot_count):

time: 330 us -> 383 us (1.16)
  waiting for transfers between devices: 265 us -> 314 us
  other arithmetic: 11.2 us -> 16.6 us
    psum x1 -> x0, waiting for transfers between devices: 56.3 us -> none  [broadcast(): return lax.psum(jnp.where(mine, shard, jnp.zeros_like(shard)), axis)]
    all_gather x0 -> x1, waiting for transfers between devices: none -> 52.8 us  [broadcast(): lax.all_gather(jnp.where(mine, shard, jnp.zeros_like(shard)), axis)]
    all_gather x1, waiting for transfers between devices: 0.03 us -> 27 us  [shards(): lax.all_gather(gate_blocks, 'fsdp', axis=2, tiled=True)]
    all_gather x1, waiting for transfers between devices: 5.83 us -> 31.3 us  [shards(): lax.all_gather(up_blocks, 'fsdp', axis=2, tiled=True)]
    reduce_sum x0 -> x1, other arithmetic: none -> 4.91 us  [broadcast(): jnp.sum(lax.all_gather(jnp.where(mine, shard, jnp.zeros_like(shard)), axi...]
  transfers between devices with their start and end apart: 8 -> 8, of which waited for: 7 -> 8; matrix products, arithmetic and copies ran while one was open for 5% -> 6% of each run, Pallas kernels for 0% -> 0%
where the time goes in v1:
time: 383 us; the launch traced here: 382 us
  waiting for transfers between devices  314 us (82%)
  local copies, waits for them, and re-layouts  22.4 us (6%)
  other arithmetic  16.6 us (4%)
  between operations  15.7 us (4%)
  matrix products  12.7 us (3%)
    psum x1, waiting for transfers between devices, shards(): lax.psum((partial_out - own_term).astype(jnp.bfloat16), 'dp')  55.9 us
    all_gather x1, waiting for transfers between devices, broadcast(): lax.all_gather(jnp.where(mine, shard, jnp.zeros_like(shard)), axis)  52.8 us
    unnamed x9, waiting for transfers between devices  51.6 us
    reduce_scatter x1, waiting for transfers between devices, shards(): lax.psum_scatter(up_grad.astype(jnp.bfloat16), 'fsdp', scatter_dimension=...  33 us
    reduce_scatter x1, waiting for transfers between devices, shards(): lax.psum_scatter(gate_grad.astype(jnp.bfloat16), 'fsdp', scatter_dimensio...  32 us
    all_gather x1, waiting for transfers between devices, shards(): lax.all_gather(up_blocks, 'fsdp', axis=2, tiled=True)  31.3 us
    all_gather x1, waiting for transfers between devices, shards(): lax.all_gather(down_blocks, 'fsdp', axis=2, tiled=True)  31 us
    all_gather x1, waiting for transfers between devices, shards(): lax.all_gather(gate_blocks, 'fsdp', axis=2, tiled=True)  27 us
  transfers between devices with their start and end apart: 8, of which 8 were waited for; matrix products, arithmetic and copies ran while one was open for 6% of the time, Pallas kernels for 0%

profile of v1, /device:TPU:0, one launch (start us, length us, event | category | flops | bytes accessed | tf_op | source)
XLA Modules:
  0.0 382.1 jit_solution(10308920849191856770)
XLA Ops:
  7.9 1.6 copy.83
  9.5 0.1 broadcast_select_fusion.3
  9.6 1.3 copy.84
  10.9 0.7 all-gather.9.cloned.1.call-update
  11.7 0.7 all-gather.11.cloned.1.call-update
  12.5 0.5 all-gather.7.cloned.1.call-update
  13.1 0.1 reshape.104
  13.1 0.1 reshape.120
  13.2 1.3 copy.96
  14.6 0.6 iota_compare_fusion
  15.2 0.1 fusion.34
  15.2 52.8 %all-gather.5.cloned.1.call-done = bf16[8,128,4096]{2,1,0:T(8,128)(2,1)} async-done(((bf16[1,128,4096]{2,1,0:T(8,128)(2,1)}), bf16[8,128,4096]{2,1,0:T(8,128)(2,1)}) %all-gather.5.cloned.1.call-update) | async-done | bytes 8388624 | tf_op jit(solution)/shard_map/all_gather | solution.py:9
  68.0 4.9 %reduce_sum.12 = bf16[128,4096]{1,0:T(8,128)(2,1)S(1)} reduce(bf16[8,128,4096]{2,1,0:T(8,128)(2,1)} %all-gather.5.cloned.1.call-done, bf16[]{:T(256)} %constant.4.clone.1), dimensions={0}, to_apply=%region_0.1 | reduce | flops 3670016 | bytes 9437186 | tf_op jit(solution)/shard_map/reduce_sum | solution.py:9
  72.9 0.7 copy.85
  73.6 0.7 copy.86
  74.3 0.8 gather_fusion
  75.1 27.0 %all-gather.9.cloned.1.call-done = bf16[4,10,128,128]{3,2,1,0:T(8,128)(2,1)} async-done(((bf16[4,10,32,128]{3,2,1,0:T(8,128)(2,1)}), bf16[4,10,128,128]{3,2,1,0:T(8,128)(2,1)}) %all-gather.9.cloned.1.call-update) | async-done | bytes 1310736 | tf_op jit(solution)/shard_map/all_gather | solution.py:35
  102.2 2.0 fusion.11
  104.1 31.3 %all-gather.11.cloned.1.call-done = bf16[4,10,128,128]{3,2,1,0:T(8,128)(2,1)} async-done(((bf16[4,10,32,128]{3,2,1,0:T(8,128)(2,1)}), bf16[4,10,128,128]{3,2,1,0:T(8,128)(2,1)}) %all-gather.11.cloned.1.call-update) | async-done | bytes 1310736 | tf_op jit(solution)/shard_map/all_gather | solution.py:36
  135.4 2.0 fusion.14
  137.4 0.1 fusion.23
  137.5 31.0 %all-gather.7.cloned.1.call-done = bf16[4,10,128,128]{3,2,1,0:T(8,128)(2,1)} async-done(((bf16[4,10,32,128]{3,2,1,0:T(8,128)(2,1)}), bf16[4,10,128,128]{3,2,1,0:T(8,128)(2,1)}) %all-gather.7.cloned.1.call-update) | async-done | bytes 1310736 | tf_op jit(solution)/shard_map/all_gather | solution.py:37
  168.5 2.0 fusion.17
  170.5 2.1 copy.94
  172.6 0.2 broadcast_in_dim.49
  172.8 6.5 %scatter_fusion = f32[128,32,128]{2,0,1:T(8,128)S(1)} fusion(f32[128,32,128]{2,0,1:T(8,128)S(1)} %broadcast_in_dim.49, s32[40]{0:T(128)S(1)} %reshape.120, f32[40,128,128]{2,1,0:T(8,128)} %copy.94), kind=kCustom, calls=%fused_computation.2 | custom fusion | flops 655360 | bytes 7864480 | tf_op jit(solution)/shard_map/scatter-add | solution.py:58
  179.4 1.8 copy.95
  181.2 2.8 fusion
  184.1 0.0 all-reduce.6.cloned.1.call-start
  184.1 55.9 %all-reduce.4.cloned.1.call-done = bf16[128,4096]{0,1:T(8,128)(2,1)} async-done(((bf16[128,4096]{0,1:T(8,128)(2,1)}), bf16[128,4096]{0,1:T(8,128)(2,1)}) %all-reduce.4.cloned.1.call-update) | async-done | bytes 1048592 | tf_op jit(solution)/shard_map/psum | solution.py:61
  240.0 1.4 multiply_convert_fusion.3
  241.5 0.7 copy.97
  242.1 0.8 gather_fusion.1
  242.9 0.8 copy.98
  243.7 1.6 fusion.1
  245.3 3.7 copy.103
  249.1 1.2 copy-done.1
  250.3 1.4 copy.87
  251.8 2.0 convolution_bitcast_fusion
  253.8 1.6 multiply_convert_fusion.2
  255.5 1.6 multiply_convert_fusion.1
  257.1 0.6 copy-done.12
  257.7 0.6 dynamic-slice
  258.9 49.6 %all-reduce.6.cloned.1.call-done = bf16[4,10,128,128]{3,0,1,2:T(4,128)(2,1)} async-done(((bf16[4,10,128,128]{3,0,1,2:T(4,128)(2,1)}), bf16[4,10,128,128]{3,0,1,2:T(4,128)(2,1)}) %all-reduce.6.cloned.1.call-update) | async-done | bytes 1310736
  308.5 1.1 constant_dynamic-slice_fusion
  309.6 0.8 copy.104
  310.4 32.0 %reduce-scatter.3.cloned.1.call-done = bf16[4,10,32,128]{3,2,1,0:T(8,128)(2,1)} async-done(((bf16[4,10,128,128]{3,2,1,0:T(8,128)(2,1)}), bf16[4,10,32,128]{3,2,1,0:T(8,128)(2,1)}) %reduce-scatter.3.cloned.1.call-update) | async-done | bytes 327696 | tf_op jit(solution)/shard_map/reduce_scatter | solution.py:88
  342.3 33.0 %reduce-scatter.5.cloned.1.call-done = bf16[4,10,32,128]{3,2,1,0:T(8,128)(2,1)} async-done(((bf16[4,10,128,128]{3,2,1,0:T(8,128)(2,1)}), bf16[4,10,32,128]{3,2,1,0:T(8,128)(2,1)}) %reduce-scatter.5.cloned.1.call-update) | async-done | bytes 327696 | tf_op jit(solution)/shard_map/reduce_scatter | solution.py:91
  (40 shorter events, 0.4 us)
Async XLA Ops:
  7.2 60.9 %all-gather.5.cloned.1.call-start = ((), (), s32[]{:S(2)}) async-start(), calls=%async_computation.2 | async-start | bytes 9437184 | tf_op jit(solution)/shard_map/all_gather | solution.py:9
  10.9 2.2 copy-start.7
  10.9 2.3 copy-start.8
  10.9 2.4 copy-start.4
  10.9 91.3 %all-gather.9.cloned.1.call-start = ((), (), s32[]{:S(2)}) async-start(), calls=%async_computation.4 | async-start | bytes 1638400 | tf_op jit(solution)/shard_map/all_gather | solution.py:35
  11.7 2.9 copy-start.9
  11.7 3.5 copy-start.10
  11.7 123.7 %all-gather.11.cloned.1.call-start = ((), (), s32[]{:S(2)}) async-start(), calls=%async_computation.5 | async-start | bytes 1638400 | tf_op jit(solution)/shard_map/all_gather | solution.py:36
  12.4 156.1 %all-gather.7.cloned.1.call-start = ((), (), s32[]{:S(2)}) async-start(), calls=%async_computation.3 | async-start | bytes 1638400 | tf_op jit(solution)/shard_map/all_gather | solution.py:37
  13.0 227.0 %all-reduce.4.cloned.1.call-start = ((), (), s32[]{:S(2)}) async-start(), calls=%async_computation.6 | async-start | bytes 2097152 | tf_op jit(solution)/shard_map/psum | solution.py:61
  74.3 27.9 %copy-start.11 = (pred[4,10]{1,0:T(4,128)(4,1)S(1)}, pred[4,10]{1,0:T(4,128)(4,1)}, u32[]{:S(2)}) copy-start(pred[4,10]{1,0:T(4,128)(4,1)} %get-tuple-element.20) | copy-start | bytes 124
  75.1 60.3 %copy-start = (bf16[40,128,128]{2,1,0:T(8,128)(2,1)}, bf16[40,128,128]{2,1,0:T(8,128)(2,1)S(1)}, u32[]{:S(2)}) copy-start(bf16[40,128,128]{2,1,0:T(8,128)(2,1)S(1)} %gather_fusion) | copy-start | bytes 3932164
  137.4 31.1 %copy-start.5 = (f32[128,4,128]{0,2,1:T(8,128)}, f32[128,4,128]{0,2,1:T(8,128)S(1)}, u32[]{:S(2)}) copy-start(f32[128,4,128]{0,2,1:T(8,128)S(1)} %fusion.14) | copy-start | bytes 786436
  179.3 1.8 copy-start.2
  184.1 124.5 %all-reduce.6.cloned.1.call-start = ((), (), s32[]{:S(2)}) async-start(), calls=%async_computation.9 | async-start | bytes 2621440
  249.0 1.3 copy-start.1
  249.0 93.3 %reduce-scatter.3.cloned.1.call-start = ((), (), s32[]{:S(2)}) async-start(), calls=%async_computation.7 | async-start | bytes 1638400 | tf_op jit(solution)/shard_map/reduce_scatter | solution.py:88
  251.8 2.0 copy-start.3
  251.8 2.0 copy-start.6
  255.4 119.9 %reduce-scatter.5.cloned.1.call-start = ((), (), s32[]{:S(2)}) async-start(), calls=%async_computation.8 | async-start | bytes 1638400 | tf_op jit(solution)/shard_map/reduce_scatter | solution.py:91
  257.0 0.7 copy-start.12
Sparse Core Ops, SparseCore 0:
  11.0 56.9 all-gather.4
  69.6 32.5 all-gather.8
  103.7 31.6 all-gather.10
  136.8 31.6 all-gather.6
  184.2 55.8 all-reduce.3
  249.2 59.3 all-reduce.5
  311.4 30.9 reduce-scatter.2
  345.2 30.0 reduce-scatter.4
